TPU v7x, 128 devices: a whole 4x4x4 slice. The times are simulated.
128 devices in a mesh: req: 16 (over x, z), head: 8 (over y, core).
Axes of the slice: x: 4, y: 4, z: 4, core: 2. Of those that a mesh axis runs over, the one named last changes fastest.
Arguments:
- hidden: bfloat16 [512, 2048], P('req', 'head'), may hold values from -6 to 6
- lengths: int32 [512], P('req'), may hold values from 1 to 384, as said below
- expert_ids: int32 [512, 8], P('req'), may hold values from 0 to 63, all different within a row
- route_weights: float32 [512, 8], P('req'), may hold values from 0.25 to 2.5
- w_qkv: bfloat16 [3, 2048, 2048], P(None, None, 'head'), may hold values from -0.125 to 0.125
- w_out: bfloat16 [2048, 2048], P('head'), may hold values from -0.125 to 0.125
- k_cache: bfloat16 [512, 384, 16, 128], P('req', None, 'head'), may hold values from -400 to 400
- v_cache: bfloat16 [512, 384, 16, 128], P('req', None, 'head'), may hold values from -12 to 12
- w_in: bfloat16 [2048, 64, 2048], P(None, 'head', 'req'), may hold values from -0.125 to 0.125
- w_down: bfloat16 [64, 1024, 2048], P('head', 'req'), may hold values from -0.1875 to 0.1875
Outputs:
- output: bfloat16 [512, 2048], P('req', 'head')
Inputs may be any that keep to these rules, and one draw needn't show every extreme that they name: `lengths`: some request has exactly 384 cached positions.
All inputs are finite; a program needn't handle non-finite values.
Results may differ from a plain program's by a relative error of at most 0.023.
Values may be sent and summed in bfloat16 or wider, within the bound.
A program may use at most 128 MiB of HBM per device.

v0:
```python
import jax
import jax.numpy as jnp
from jax import lax
from jax.sharding import PartitionSpec as P

UNIT_BLOCK = 64
KEY_BLOCK = 128
rope_theta = 50000.0
norm_eps = 1e-05


def over_all(shard, axis, dim, work):
    return work(lax.all_gather(shard, axis, axis=dim, tiled=True), jnp.int32(0))


def rotate(values, positions):
    half_dim = values.shape[-1] // 2
    freqs = rope_theta ** (-jnp.arange(half_dim, dtype=jnp.float32) / half_dim)
    angles = positions.astype(jnp.float32)[:, None] * freqs[None, :]
    cosine = jnp.cos(angles)[:, None, :]
    sine = jnp.sin(angles)[:, None, :]
    first_half = values[..., :half_dim]
    second_half = values[..., half_dim:]
    return jnp.concatenate(
        [first_half * cosine - second_half * sine, second_half * cosine + first_half * sine],
        axis=-1,
    )


def rms_normed(values):
    return (
        values * lax.rsqrt(jnp.mean(values * values, axis=-1, keepdims=True) + norm_eps)
    ).astype(jnp.bfloat16)


def per_device(
    hidden, lengths, expert_ids, route_weights, w_qkv, w_out, k_cache, v_cache, w_in, w_down
):
    full_rows = lax.all_gather(hidden, "head", axis=1, tiled=True)
    hidden_f = full_rows.astype(jnp.float32)
    normed = rms_normed(hidden_f)
    req_local = hidden.shape[0]
    col_width = hidden.shape[1]
    heads_local = k_cache.shape[2]
    head_size = k_cache.shape[3]
    cache_len = k_cache.shape[1]
    projected = jnp.einsum("td,cdn->ctn", normed, w_qkv, preferred_element_type=jnp.float32)
    projected = projected.reshape(3, req_local, heads_local, head_size)
    query = rotate(projected[0], lengths).astype(jnp.bfloat16)
    key_new = rotate(projected[1], lengths).astype(jnp.bfloat16)
    value_new = projected[2].astype(jnp.bfloat16)
    score_scale = head_size ** (-0.5)
    block_count = (jnp.max(lengths) + KEY_BLOCK - 1) // KEY_BLOCK

    def score_block(block_idx, buffer):
        keys_block = lax.dynamic_slice_in_dim(k_cache, block_idx * KEY_BLOCK, KEY_BLOCK, 1)
        block_scores = (
            jnp.einsum("rhd,rlhd->rhl", query, keys_block, preferred_element_type=jnp.float32)
            * score_scale
        )
        return lax.dynamic_update_slice_in_dim(buffer, block_scores, block_idx * KEY_BLOCK, 2)

    buffer = jnp.full((req_local, heads_local, cache_len), -jnp.inf, jnp.float32)
    buffer = lax.fori_loop(0, block_count, score_block, buffer)
    positions = jnp.arange(cache_len, dtype=jnp.int32)
    scores = jnp.where(positions[None, None, :] < lengths[:, None, None], buffer, -jnp.inf)
    self_score = (
        jnp.einsum("rhd,rhd->rh", query, key_new, preferred_element_type=jnp.float32) * score_scale
    )
    row_top = jnp.maximum(jnp.max(scores, axis=-1), self_score)
    exponent = jnp.exp(scores - row_top[:, :, None])
    self_exp = jnp.exp(self_score - row_top)
    denominator = jnp.sum(exponent, axis=-1) + self_exp
    weights = (exponent / denominator[:, :, None]).astype(jnp.bfloat16)
    self_weight = (self_exp / denominator).astype(jnp.bfloat16)

    def value_block(block_idx, accum):
        weights_block = lax.dynamic_slice_in_dim(weights, block_idx * KEY_BLOCK, KEY_BLOCK, 2)
        values_block = lax.dynamic_slice_in_dim(v_cache, block_idx * KEY_BLOCK, KEY_BLOCK, 1)
        return accum + jnp.einsum(
            "rhl,rlhd->rhd", weights_block, values_block, preferred_element_type=jnp.float32
        )

    accum = lax.fori_loop(
        0, block_count, value_block, jnp.zeros((req_local, heads_local, head_size), jnp.float32)
    )
    accum = accum + self_weight.astype(jnp.float32)[:, :, None] * value_new.astype(jnp.float32)
    attended = accum.astype(jnp.bfloat16).reshape(req_local, heads_local * head_size)
    head_terms = jnp.dot(attended, w_out, preferred_element_type=jnp.float32)
    resid = hidden_f + lax.psum(head_terms.astype(jnp.bfloat16), "head").astype(jnp.float32)
    mixed = rms_normed(resid)
    experts_local = w_down.shape[0]
    units_local = w_down.shape[1]
    width = w_in.shape[0]
    expert_base = lax.axis_index("head") * experts_local + jnp.arange(
        experts_local, dtype=jnp.int32
    )
    w_in_flat = w_in.reshape(width, experts_local * 2 * units_local)
    w_down_flat = w_down.reshape(experts_local * units_local, width)

    def expert_hidden(pieces):
        token_rows, token_ids, token_weights = pieces
        row_count = token_rows.shape[0]
        matches = (token_ids[:, :, None] == expert_base[None, None, :]).astype(jnp.float32)
        combined = jnp.sum(token_weights[:, :, None] * matches, axis=1)
        gate_up = jnp.dot(token_rows, w_in_flat, preferred_element_type=jnp.float32)
        gate_up = gate_up.reshape(
            row_count, experts_local, units_local // UNIT_BLOCK, 2, UNIT_BLOCK
        )
        gate = gate_up[:, :, :, 0, :]
        upward = gate_up[:, :, :, 1, :]
        units = (combined[:, :, None, None] * (jax.nn.silu(gate) * upward)).astype(jnp.bfloat16)
        return units.reshape(row_count, experts_local * units_local)

    gathered = over_all(
        (mixed, expert_ids, route_weights.astype(jnp.bfloat16)),
        "req",
        0,
        lambda piece, start: expert_hidden((piece[0], piece[1], piece[2].astype(jnp.float32))),
    )
    token_sums = lax.psum_scatter(
        jnp.dot(gathered, w_down_flat, preferred_element_type=jnp.float32).astype(jnp.bfloat16),
        "req",
        scatter_dimension=0,
        tiled=True,
    )
    moe_share = lax.psum_scatter(token_sums, "head", scatter_dimension=1, tiled=True).astype(
        jnp.float32
    )
    resid_share = lax.dynamic_slice_in_dim(resid, lax.axis_index("head") * col_width, col_width, 1)
    return (resid_share + moe_share).astype(jnp.bfloat16)


def solution(mesh):
    in_specs = (
        P("req", "head"),
        P("req"),
        P("req", None),
        P("req", None),
        P(None, None, "head"),
        P("head", None),
        P("req", None, "head", None),
        P("req", None, "head", None),
        P(None, "head", "req"),
        P("head", "req", None),
    )
    out_specs = P("req", "head")
    return jax.shard_map(
        per_device, mesh=mesh, in_specs=in_specs, out_specs=out_specs, check_vma=False
    )
```

profile of v0, /device:TPU:0, one launch (start us, length us, event | category | flops | bytes accessed | tf_op | source)
XLA Modules:
  0.0 295.3 jit_solution(10941780529254591769)
XLA Ops:
  6.5 1.5 fusion.28
  9.5 13.6 %all_gather.12 = bf16[32,2048]{1,0:T(8,128)(2,1)S(1)} all-gather(bf16[32,256]{1,0:T(8,128)(2,1)} %param.14), channel_id=1, replica_groups=mesh['req'=16,'head'=8] {'head'}, dimensions={1}, use_global_device_ids=true | all-gather | bytes 147456 | tf_op jit(solution)/shard_map/all_gather | solution.py:39
  24.6 13.6 %while.20 = (s32[]{:T(128)}, f32[32,2,384]{2,1,0:T(2,128)S(1)}, s32[]{:T(128)}, bf16[32,384,2,128]{3,2,1,0:T(2,128)(2,1)}, bf16[32,2,128]{2,1,0:T(2,128)(2,1)S(1...) while((s32[]{:T(128)}, f32[32,2,384]{2,1,0:T(2,128)S(1)}, s32[]{:T(128)}, ...), condition=%wide.region_3.4_spmd, body=%wide.region_2.3_spmd.sunk | while | flops 2105350 | bytes 6406299 | solution.py:64
  24.6 3.3 %constant_dynamic-slice_fusion.4 = bf16[32,128,2,128]{3,2,1,0:T(2,128)(2,1)S(1)} fusion(bf16[32,384,2,128]{3,2,1,0:T(2,128)(2,1)} %get-tuple-element.186, s32[]{:T(128)S(6)} %select_n.34), kind=kLoop, calls=%fused_computation.4.clone.1 | loop fusion | bytes 4194308 | tf_op jit(solution)/shard_map/while/body/dynamic_slice | solution.py:56
  27.9 1.2 fusion.42
  29.2 3.3 %constant_dynamic-slice_fusion.4 = bf16[32,128,2,128]{3,2,1,0:T(2,128)(2,1)S(1)} fusion(bf16[32,384,2,128]{3,2,1,0:T(2,128)(2,1)} %get-tuple-element.186, s32[]{:T(128)S(6)} %select_n.34), kind=kLoop, calls=%fused_computation.4.clone.1 | loop fusion | bytes 4194308 | tf_op jit(solution)/shard_map/while/body/dynamic_slice | solution.py:56
  33.7 3.3 %constant_dynamic-slice_fusion.4 = bf16[32,128,2,128]{3,2,1,0:T(2,128)(2,1)S(1)} fusion(bf16[32,384,2,128]{3,2,1,0:T(2,128)(2,1)} %get-tuple-element.186, s32[]{:T(128)S(6)} %select_n.34), kind=kLoop, calls=%fused_computation.4.clone.1 | loop fusion | bytes 4194308 | tf_op jit(solution)/shard_map/while/body/dynamic_slice | solution.py:56
  38.9 12.1 %while.21 = (s32[]{:T(128)}, f32[32,2,128]{2,1,0:T(2,128)S(1)}, s32[]{:T(128)}, bf16[32,2,384]{2,1,0:T(2,128)(2,1)S(1)}, bf16[32,384,2,128]{3,2,1,0:T(2,128)(2,1...) while((s32[]{:T(128)}, f32[32,2,128]{2,1,0:T(2,128)S(1)}, s32[]{:T(128)}, ...), condition=%wide.region_7.8_spmd, body=%wide.region_6.7_spmd.sunk | while | flops 2105350 | bytes 6471835 | solution.py:84
  38.9 3.3 %constant_dynamic-slice_fusion.5 = bf16[32,128,2,128]{3,2,1,0:T(2,128)(2,1)S(1)} fusion(bf16[32,384,2,128]{3,2,1,0:T(2,128)(2,1)} %get-tuple-element.214, s32[]{:T(128)S(6)} %select_n.35), kind=kLoop, calls=%fused_computation.9.clone.1 | loop fusion | bytes 4194308 | tf_op jit(solution)/shard_map/while/body/dynamic_slice | solution.py:79
  42.9 3.3 %constant_dynamic-slice_fusion.5 = bf16[32,128,2,128]{3,2,1,0:T(2,128)(2,1)S(1)} fusion(bf16[32,384,2,128]{3,2,1,0:T(2,128)(2,1)} %get-tuple-element.214, s32[]{:T(128)S(6)} %select_n.35), kind=kLoop, calls=%fused_computation.9.clone.1 | loop fusion | bytes 4194308 | tf_op jit(solution)/shard_map/while/body/dynamic_slice | solution.py:79
  46.9 3.3 %constant_dynamic-slice_fusion.5 = bf16[32,128,2,128]{3,2,1,0:T(2,128)(2,1)S(1)} fusion(bf16[32,384,2,128]{3,2,1,0:T(2,128)(2,1)} %get-tuple-element.214, s32[]{:T(128)S(6)} %select_n.35), kind=kLoop, calls=%fused_computation.9.clone.1 | loop fusion | bytes 4194308 | tf_op jit(solution)/shard_map/while/body/dynamic_slice | solution.py:79
  51.1 2.2 convolution_convert_fusion.1
  53.3 60.9 %all-reduce.2.cloned.1.call-done = bf16[32,2048]{1,0:T(8,128)(2,1)} async-done(((bf16[32,2048]{1,0:T(8,128)(2,1)}), bf16[32,2048]{1,0:T(8,128)(2,1)}) %all-reduce.2.cloned.1.call-update) | async-done | bytes 131088 | tf_op jit(solution)/shard_map/psum | solution.py:90
  115.3 1.6 multiply_convert_fusion
  117.0 5.3 %copy.57 = bf16[256,8,8,128]{3,1,2,0:T(8,128)(2,1)} copy(bf16[256,8,8,128]{3,2,1,0:T(8,128)(2,1)} %bitcast.70) | data formatting | bytes 8388608
  122.3 6.5 %copy.27 = bf16[1024,2048]{1,0:T(8,128)(2,1)} copy(bf16[1024,2048]{0,1:T(8,128)(2,1)} %bitcast.69) | data formatting | bytes 8388608 | tf_op jit(solution)/shard_map/dot_general | solution.py:106
  128.8 23.5 %all-gather.1 = bf16[16,32,8]{1,2,0:T(8,128)(2,1)S(1)} all-gather(bf16[1,32,8]{1,2,0:T(8,128)(2,1)S(1)} %convert_bitcast_fusion), channel_id=1, replica_groups=mesh['req'=16,'head'=8] {'req'}, dimensions={0}, use_global_device_ids=true | all-gather | bytes 8704 | tf_op jit(solution)/shard_map/all_gather | solution.py:13
  152.4 23.1 %all-gather = s32[16,32,8]{1,2,0:T(8,128)S(1)} all-gather(s32[1,32,8]{1,2,0:T(8,128)} %bitcast.77), channel_id=1, replica_groups=mesh['req'=16,'head'=8] {'req'}, dimensions={0}, use_global_device_ids=true | all-gather | bytes 17408 | tf_op jit(solution)/shard_map/all_gather | solution.py:13
  175.8 5.2 %fusion.8 = f32[512,8,1,2,64]{0,4,3,1,2:T(8,128)S(1)} fusion(bf16[8,2,64,2048]{3,2,1,0:T(8,128)(2,1)} %bitcast.71, bf16[512,2048]{1,0:T(8,128)(2,1)} %all-gather.4.cloned.1.call-done), kind=kOutput, calls=%fused_computation.15 | convolution fusion | flops 2147483648 | bytes 8388608 | tf_op jit(solution)/shard_map/dot_general | solution.py:106
  181.3 1.2 copy-done.2
  182.6 2.6 convolution_convert_fusion
  185.3 70.5 %reduce-scatter.3.cloned.1.call-done = bf16[32,2048]{1,0:T(8,128)(2,1)} async-done(((bf16[512,2048]{1,0:T(8,128)(2,1)}), bf16[32,2048]{1,0:T(8,128)(2,1)}) %reduce-scatter.3.cloned.1.call-update) | async-done | bytes 131088 | tf_op jit(solution)/shard_map/reduce_scatter | solution.py:121
  255.8 31.7 %reduce-scatter.5.cloned.1.call-done = bf16[32,256]{1,0:T(8,128)(2,1)} async-done(((bf16[32,2048]{1,0:T(8,128)(2,1)}), bf16[32,256]{1,0:T(8,128)(2,1)}) %reduce-scatter.5.cloned.1.call-update) | async-done | bytes 16400 | tf_op jit(solution)/shard_map/reduce_scatter | solution.py:127
  287.5 1.3 add_convert_fusion
  (59 shorter events, 9.4 us)
Async XLA Ops:
  6.5 16.7 %copy-start = (bf16[3,2048,256]{2,1,0:T(8,128)(2,1)S(1)}, bf16[3,2048,256]{2,1,0:T(8,128)(2,1)}, u32[]{:S(2)}) copy-start(bf16[3,2048,256]{2,1,0:T(8,128)(2,1)} %param.18) | copy-start | bytes 9437188
  6.5 107.7 %all-reduce.2.cloned.1.call-start = ((), (), s32[]{:S(2)}) async-start(), calls=%async_computation.2 | async-start | bytes 262144 | tf_op jit(solution)/shard_map/psum | solution.py:90
  53.3 122.5 %all-gather.4.cloned.1.call-start = ((), (), s32[]{:S(2)}) async-start(), calls=%async_computation.3 | async-start | bytes 2228224 | tf_op jit(solution)/shard_map/all_gather | solution.py:13
  117.0 138.8 %reduce-scatter.3.cloned.1.call-start = ((), (), s32[]{:S(2)}) async-start(), calls=%async_computation.4 | async-start | bytes 2228224 | tf_op jit(solution)/shard_map/reduce_scatter | solution.py:121
  122.3 6.5 %copy-start.1 = (f32[32,8]{0,1:T(8,128)S(1)}, f32[32,8]{0,1:T(8,128)}, u32[]{:S(2)}) copy-start(f32[32,8]{0,1:T(8,128)} %param.17) | copy-start | bytes 3076
  181.0 1.6 copy-start.2
  185.2 102.3 %reduce-scatter.5.cloned.1.call-start = ((), (), s32[]{:S(2)}) async-start(), calls=%async_computation.5 | async-start | bytes 147456 | tf_op jit(solution)/shard_map/reduce_scatter | solution.py:127
Sparse Core Ops, SparseCore 0:
  53.4 60.8 all-reduce.1
  117.1 44.3 all-gather.3
  185.4 70.3 reduce-scatter.2
  258.0 29.4 reduce-scatter.4
where the time goes:
time: 296 us; the launch traced here: 295 us
  waiting for transfers between devices  163 us (55%)
  blocking collectives  60.2 us (20%)
  local copies, waits for them, and re-layouts  33.1 us (11%)
  matrix products  16.1 us (5%)
  between operations  14 us (5%)
  other arithmetic  8.33 us (3%)
    reduce_scatter x1, waiting for transfers between devices, per_device(): lax.psum_scatter(jnp.dot(gathered, w_down_flat, preferred_element_type=jn...  70.5 us
    psum x1, waiting for transfers between devices, per_device(): lax.psum(head_terms.astype(jnp.bfloat16), 'head').astype(jnp.float32)  60.9 us
    all_gather x2, blocking collectives, over_all(): return work(lax.all_gather(shard, axis, axis=dim, tiled=True), jnp.int32(0))  46.6 us
    reduce_scatter x1, waiting for transfers between devices, per_device(): lax.psum_scatter(token_sums, 'head', scatter_dimension=1, tiled=True)  31.7 us
    all_gather x1, blocking collectives, per_device(): full_rows = lax.all_gather(hidden, 'head', axis=1, tiled=True)  13.6 us
    dynamic_slice x3, local copies, waits for them, and re-layouts, score_block(): lax.dynamic_slice_in_dim(k_cache, block_idx * KEY_BLOCK, KEY_BLOCK, 1)  9.85 us
    dynamic_slice x3, local copies, waits for them, and re-layouts, value_block(): lax.dynamic_slice_in_dim(v_cache, block_idx * KEY_BLOCK, KEY_BLOCK, 1)  9.85 us
    unnamed x8, local copies, waits for them, and re-layouts  6.58 us
  transfers between devices with their start and end apart: 4, of which 3 were waited for; matrix products, arithmetic and copies ran while one was open for 4% of the time, Pallas kernels for 0%

commit v1 on v0

--- a/solution.py
+++ b/solution.py
@@ -87,7 +87,9 @@
     accum = accum + self_weight.astype(jnp.float32)[:, :, None] * value_new.astype(jnp.float32)
     attended = accum.astype(jnp.bfloat16).reshape(req_local, heads_local * head_size)
     head_terms = jnp.dot(attended, w_out, preferred_element_type=jnp.float32)
-    resid = hidden_f + lax.psum(head_terms.astype(jnp.bfloat16), "head").astype(jnp.float32)
+    resid = hidden_f + jnp.sum(
+        lax.all_gather(head_terms.astype(jnp.bfloat16), "head"), axis=0
+    ).astype(jnp.float32)
     mixed = rms_normed(resid)
     experts_local = w_down.shape[0]
     units_local = w_down.shape[1]

time: 296 us -> 262 us (0.89)
  waiting for transfers between devices: 163 us -> 128 us
    psum x1 -> x0, waiting for transfers between devices: 60.9 us -> none  [per_device(): lax.psum(head_terms.astype(jnp.bfloat16), 'head').astype(jnp.float32)]
    all_gather x0 -> x1, waiting for transfers between devices: none -> 25 us  [per_device(): lax.all_gather(head_terms.astype(jnp.bfloat16), 'head')]
    unnamed x8 -> x10, local copies, waits for them, and re-layouts: 6.58 us -> 6.59 us
  transfers between devices with their start and end apart: 4 -> 4, of which waited for: 3 -> 3; matrix products, arithmetic and copies ran while one was open for 4% -> 5% of each run, Pallas kernels for 0% -> 0%
where the time goes in v1:
time: 262 us; the launch traced here: 261 us
  waiting for transfers between devices  128 us (49%)
  blocking collectives  60.2 us (23%)
  local copies, waits for them, and re-layouts  33.1 us (13%)
  matrix products  16.1 us (6%)
  between operations  14.1 us (5%)
  other arithmetic  8.68 us (3%)
    reduce_scatter x1, waiting for transfers between devices, per_device(): lax.psum_scatter(jnp.dot(gathered, w_down_flat, preferred_element_type=jn...  71.5 us
    all_gather x2, blocking collectives, over_all(): return work(lax.all_gather(shard, axis, axis=dim, tiled=True), jnp.int32(0))  46.6 us
    reduce_scatter x1, waiting for transfers between devices, per_device(): lax.psum_scatter(token_sums, 'head', scatter_dimension=1, tiled=True)  31.8 us
    all_gather x1, waiting for transfers between devices, per_device(): lax.all_gather(head_terms.astype(jnp.bfloat16), 'head')  25 us
    all_gather x1, blocking collectives, per_device(): full_rows = lax.all_gather(hidden, 'head', axis=1, tiled=True)  13.6 us
    dynamic_slice x3, local copies, waits for them, and re-layouts, score_block(): lax.dynamic_slice_in_dim(k_cache, block_idx * KEY_BLOCK, KEY_BLOCK, 1)  9.85 us
    dynamic_slice x3, local copies, waits for them, and re-layouts, value_block(): lax.dynamic_slice_in_dim(v_cache, block_idx * KEY_BLOCK, KEY_BLOCK, 1)  9.85 us
    unnamed x10, local copies, waits for them, and re-layouts  6.59 us
  transfers between devices with their start and end apart: 4, of which 3 were waited for; matrix products, arithmetic and copies ran while one was open for 5% of the time, Pallas kernels for 0%

profile of v1, /device:TPU:0, one launch (start us, length us, event | category | flops | bytes accessed | tf_op | source)
XLA Modules:
  0.0 260.9 jit_solution(17952878895754750406)
XLA Ops:
  6.5 1.5 fusion.28
  9.5 13.6 %all_gather.18 = bf16[32,2048]{1,0:T(8,128)(2,1)S(1)} all-gather(bf16[32,256]{1,0:T(8,128)(2,1)} %param.14), channel_id=1, replica_groups=mesh['req'=16,'head'=8] {'head'}, dimensions={1}, use_global_device_ids=true | all-gather | bytes 147456 | tf_op jit(solution)/shard_map/all_gather | solution.py:39
  24.6 13.6 %while.20 = (s32[]{:T(128)}, f32[32,2,384]{2,1,0:T(2,128)S(1)}, s32[]{:T(128)}, bf16[32,384,2,128]{3,2,1,0:T(2,128)(2,1)}, bf16[32,2,128]{2,1,0:T(2,128)(2,1)S(1...) while((s32[]{:T(128)}, f32[32,2,384]{2,1,0:T(2,128)S(1)}, s32[]{:T(128)}, ...), condition=%wide.region_3.4_spmd, body=%wide.region_2.3_spmd.sunk | while | flops 2105350 | bytes 6406299 | solution.py:64
  24.6 3.3 %constant_dynamic-slice_fusion.4 = bf16[32,128,2,128]{3,2,1,0:T(2,128)(2,1)S(1)} fusion(bf16[32,384,2,128]{3,2,1,0:T(2,128)(2,1)} %get-tuple-element.186, s32[]{:T(128)S(6)} %select_n.34), kind=kLoop, calls=%fused_computation.4.clone.1 | loop fusion | bytes 4194308 | tf_op jit(solution)/shard_map/while/body/dynamic_slice | solution.py:56
  27.9 1.2 fusion.42
  29.2 3.3 %constant_dynamic-slice_fusion.4 = bf16[32,128,2,128]{3,2,1,0:T(2,128)(2,1)S(1)} fusion(bf16[32,384,2,128]{3,2,1,0:T(2,128)(2,1)} %get-tuple-element.186, s32[]{:T(128)S(6)} %select_n.34), kind=kLoop, calls=%fused_computation.4.clone.1 | loop fusion | bytes 4194308 | tf_op jit(solution)/shard_map/while/body/dynamic_slice | solution.py:56
  33.7 3.3 %constant_dynamic-slice_fusion.4 = bf16[32,128,2,128]{3,2,1,0:T(2,128)(2,1)S(1)} fusion(bf16[32,384,2,128]{3,2,1,0:T(2,128)(2,1)} %get-tuple-element.186, s32[]{:T(128)S(6)} %select_n.34), kind=kLoop, calls=%fused_computation.4.clone.1 | loop fusion | bytes 4194308 | tf_op jit(solution)/shard_map/while/body/dynamic_slice | solution.py:56
  38.9 12.1 %while.21 = (s32[]{:T(128)}, f32[32,2,128]{2,1,0:T(2,128)S(1)}, s32[]{:T(128)}, bf16[32,2,384]{2,1,0:T(2,128)(2,1)S(1)}, bf16[32,384,2,128]{3,2,1,0:T(2,128)(2,1...) while((s32[]{:T(128)}, f32[32,2,128]{2,1,0:T(2,128)S(1)}, s32[]{:T(128)}, ...), condition=%wide.region_7.8_spmd, body=%wide.region_6.7_spmd.sunk | while | flops 2105350 | bytes 6471835 | solution.py:84
  38.9 3.3 %constant_dynamic-slice_fusion.5 = bf16[32,128,2,128]{3,2,1,0:T(2,128)(2,1)S(1)} fusion(bf16[32,384,2,128]{3,2,1,0:T(2,128)(2,1)} %get-tuple-element.214, s32[]{:T(128)S(6)} %select_n.35), kind=kLoop, calls=%fused_computation.9.clone.1 | loop fusion | bytes 4194308 | tf_op jit(solution)/shard_map/while/body/dynamic_slice | solution.py:79
  42.9 3.3 %constant_dynamic-slice_fusion.5 = bf16[32,128,2,128]{3,2,1,0:T(2,128)(2,1)S(1)} fusion(bf16[32,384,2,128]{3,2,1,0:T(2,128)(2,1)} %get-tuple-element.214, s32[]{:T(128)S(6)} %select_n.35), kind=kLoop, calls=%fused_computation.9.clone.1 | loop fusion | bytes 4194308 | tf_op jit(solution)/shard_map/while/body/dynamic_slice | solution.py:79
  46.9 3.3 %constant_dynamic-slice_fusion.5 = bf16[32,128,2,128]{3,2,1,0:T(2,128)(2,1)S(1)} fusion(bf16[32,384,2,128]{3,2,1,0:T(2,128)(2,1)} %get-tuple-element.214, s32[]{:T(128)S(6)} %select_n.35), kind=kLoop, calls=%fused_computation.9.clone.1 | loop fusion | bytes 4194308 | tf_op jit(solution)/shard_map/while/body/dynamic_slice | solution.py:79
  51.1 2.2 convolution_convert_fusion.1
  53.3 25.0 %all-gather.8.cloned.1.call-done = bf16[256,2048]{1,0:T(8,128)(2,1)} async-done(((bf16[32,2048]{1,0:T(8,128)(2,1)}), bf16[256,2048]{1,0:T(8,128)(2,1)}) %all-gather.8.cloned.1.call-update) | async-done | bytes 1048592 | tf_op jit(solution)/shard_map/all_gather | solution.py:91
  78.3 1.4 reduce_sum.50
  81.4 5.3 %copy.57 = bf16[256,8,8,128]{3,1,2,0:T(8,128)(2,1)} copy(bf16[256,8,8,128]{3,2,1,0:T(8,128)(2,1)} %bitcast.71) | data formatting | bytes 8388608
  86.7 6.5 %copy.27 = bf16[1024,2048]{1,0:T(8,128)(2,1)} copy(bf16[1024,2048]{0,1:T(8,128)(2,1)} %bitcast.70) | data formatting | bytes 8388608 | tf_op jit(solution)/shard_map/dot_general | solution.py:108
  93.2 23.5 %all-gather.2 = bf16[16,32,8]{1,2,0:T(8,128)(2,1)S(1)} all-gather(bf16[1,32,8]{1,2,0:T(8,128)(2,1)S(1)} %convert_bitcast_fusion), channel_id=1, replica_groups=mesh['req'=16,'head'=8] {'req'}, dimensions={0}, use_global_device_ids=true | all-gather | bytes 8704 | tf_op jit(solution)/shard_map/all_gather | solution.py:13
  116.8 23.1 %all-gather.1 = s32[16,32,8]{1,2,0:T(8,128)S(1)} all-gather(s32[1,32,8]{1,2,0:T(8,128)S(1)} %bitcast.79), channel_id=1, replica_groups=mesh['req'=16,'head'=8] {'req'}, dimensions={0}, use_global_device_ids=true | all-gather | bytes 17408 | tf_op jit(solution)/shard_map/all_gather | solution.py:13
  140.2 5.2 %fusion.8 = f32[512,8,1,2,64]{0,4,3,1,2:T(8,128)S(1)} fusion(bf16[8,2,64,2048]{3,2,1,0:T(8,128)(2,1)} %bitcast.72, bf16[512,2048]{1,0:T(8,128)(2,1)} %all-gather.6.cloned.1.call-done), kind=kOutput, calls=%fused_computation.15 | convolution fusion | flops 2147483648 | bytes 8388608 | tf_op jit(solution)/shard_map/dot_general | solution.py:108
  145.7 1.2 copy-done.3
  147.0 2.6 %convolution_convert_fusion = bf16[512,2048]{1,0:T(8,128)(2,1)} fusion(bf16[512,512]{0,1:T(8,128)(2,1)S(1)} %bitcast.76, bf16[512,2048]{1,0:T(8,128)(2,1)S(1)} %bitcast.80), kind=kOutput, calls=%fused_computation.11 | convolution fusion | flops 1074790400 | bytes 4718592 | tf_op jit(solution)/shard_map/dot_general | solution.py:124
  149.7 71.5 %reduce-scatter.3.cloned.1.call-done = bf16[32,2048]{1,0:T(8,128)(2,1)} async-done(((bf16[512,2048]{1,0:T(8,128)(2,1)}), bf16[32,2048]{1,0:T(8,128)(2,1)}) %reduce-scatter.3.cloned.1.call-update) | async-done | bytes 131088 | tf_op jit(solution)/shard_map/reduce_scatter | solution.py:123
  221.2 31.8 %reduce-scatter.5.cloned.1.call-done = bf16[32,256]{1,0:T(8,128)(2,1)} async-done(((bf16[32,2048]{1,0:T(8,128)(2,1)}), bf16[32,256]{1,0:T(8,128)(2,1)}) %reduce-scatter.5.cloned.1.call-update) | async-done | bytes 16400 | tf_op jit(solution)/shard_map/reduce_scatter | solution.py:129
  253.0 1.4 add_convert_fusion
  (62 shorter events, 9.9 us)
Async XLA Ops:
  6.5 16.7 %copy-start = (bf16[3,2048,256]{2,1,0:T(8,128)(2,1)S(1)}, bf16[3,2048,256]{2,1,0:T(8,128)(2,1)}, u32[]{:S(2)}) copy-start(bf16[3,2048,256]{2,1,0:T(8,128)(2,1)} %param.18) | copy-start | bytes 9437188
  6.5 71.8 %all-gather.8.cloned.1.call-start = ((), (), s32[]{:S(2)}) async-start(), calls=%async_computation.5 | async-start | bytes 1179648 | tf_op jit(solution)/shard_map/all_gather | solution.py:91
  53.3 86.9 %all-gather.6.cloned.1.call-start = ((), (), s32[]{:S(2)}) async-start(), calls=%async_computation.2 | async-start | bytes 2228224 | tf_op jit(solution)/shard_map/all_gather | solution.py:13
  81.4 139.8 %reduce-scatter.3.cloned.1.call-start = ((), (), s32[]{:S(2)}) async-start(), calls=%async_computation.3 | async-start | bytes 2228224 | tf_op jit(solution)/shard_map/reduce_scatter | solution.py:123
  86.7 6.5 %copy-start.2 = (f32[32,8]{0,1:T(8,128)S(1)}, f32[32,8]{0,1:T(8,128)}, u32[]{:S(2)}) copy-start(f32[32,8]{0,1:T(8,128)} %param.17) | copy-start | bytes 3076
  86.7 30.1 %copy-start.1 = (s32[32,8]{0,1:T(8,128)S(1)}, s32[32,8]{0,1:T(8,128)}, u32[]{:S(2)}) copy-start(s32[32,8]{0,1:T(8,128)} %param.16) | copy-start | bytes 3076
  145.4 1.6 copy-start.3
  149.6 103.4 %reduce-scatter.5.cloned.1.call-start = ((), (), s32[]{:S(2)}) async-start(), calls=%async_computation.4 | async-start | bytes 147456 | tf_op jit(solution)/shard_map/reduce_scatter | solution.py:129
Sparse Core Ops, SparseCore 0:
  53.4 24.8 all-gather.7
  81.5 45.1 all-gather.5
  149.7 71.3 reduce-scatter.2
  223.5 29.4 reduce-scatter.4
